TPU v7x, 32 devices: a whole 2x2x4 slice. The times are simulated.
32 devices in a mesh: beam: 2 (over y), inp: 8 (over z, x), span: 2 (over core).
Axes of the slice: x: 2, y: 2, z: 4, core: 2. Of those that a mesh axis runs over, the one named last changes fastest.
Arguments:
- voltages: bfloat16 [2, 8, 1024, 16384], P(None, 'beam', 'inp', 'span'), parts along dimension 1, may hold values from -6 to 6
- gains: float32 [2, 8, 1024, 32], P(None, 'beam', 'inp'), parts along dimension 1, may hold values from -4 to 4
Outputs:
- visibilities: bfloat16 [256, 1024, 1024], P(('beam', 'inp'), 'span'), parts along dimension 0
There are 2 independent parts, one for each index of `beam`. A program takes and returns all parts, laid end to end along the dimension named above; each array names one. Nothing has to cross between parts.
All inputs are finite; a program needn't handle non-finite values.
Results may differ from a plain program's by a relative error of at most 0.0085.
Values may be sent and summed in bfloat16 or wider, within the bound.
A program may use at most 192 MiB of HBM per device.

v0:
```python
import math
import jax
import jax.numpy as jnp
from jax import lax
from jax.sharding import PartitionSpec as P

FINE = 32
TAPS = 4


def prototype(tap_count, fine_count):
    length = tap_count * fine_count
    offsets = jnp.arange(length).astype(jnp.float32)
    shifted = (offsets - length / 2 + 0.5) / fine_count
    taper = 0.5 - 0.5 * jnp.cos(2.0 * math.pi * (offsets + 0.5) / length)
    window = jnp.sinc(shifted) * taper
    window = window / jnp.sqrt(jnp.sum(window * window))
    return window.reshape(tap_count, fine_count)


def kernels(window, fine_count):
    points = jnp.arange(fine_count)
    phase_steps = points[:, None] * points[None, :] % fine_count
    angles = 2.0 * math.pi * phase_steps.astype(jnp.float32) / fine_count
    cosine = jnp.cos(angles)
    sine_part = jnp.sin(angles)
    result = []
    for tap_index in range(window.shape[0]):
        weights = window[tap_index][:, None]
        hcos = weights * cosine
        hsin = weights * sine_part
        result.append(jnp.stack([jnp.stack([hcos, -hsin]), jnp.stack([hsin, hcos])]))
    return jnp.stack(result)


def packed_rows(left_rows, right_rows, left_all, row_start):
    real_sums = jnp.einsum("cif,cjf->cij", left_rows, left_all, preferred_element_type=jnp.float32)
    imag_sums = jnp.einsum("cif,cjf->cij", right_rows, left_all, preferred_element_type=jnp.float32)
    row_index = row_start + jnp.arange(left_rows.shape[1])
    col_index = jnp.arange(left_all.shape[1])
    upper = row_index[:, None] <= col_index[None, :]
    return jnp.where(upper[None], real_sums, imag_sums)


def local(voltages, gains):
    coarse = voltages.shape[1]
    local_inputs = voltages.shape[2]
    samples = voltages.shape[3]
    frames = samples // FINE
    window = prototype(TAPS, FINE)
    filters = kernels(window, FINE)
    filter_table = jnp.transpose(filters, (1, 0, 3, 2, 4))
    filter_high = filter_table.astype(jnp.bfloat16)
    filter_low = (filter_table - filter_high.astype(jnp.float32)).astype(jnp.bfloat16)
    padded = jnp.pad(voltages, ((0, 0), (0, 0), (0, 0), (0, (TAPS - 1) * FINE)))
    stacked = jnp.stack(
        [padded[..., tap_index * FINE : tap_index * FINE + samples] for tap_index in range(TAPS)],
        axis=1,
    )
    stacked = stacked.reshape(2, TAPS, coarse, local_inputs, frames, FINE)
    spectra = jnp.einsum(
        "atcnmp,atpbk->bcknm", stacked, filter_high, preferred_element_type=jnp.float32
    )
    spectra = spectra + jnp.einsum(
        "atcnmp,atpbk->bcknm", stacked, filter_low, preferred_element_type=jnp.float32
    )
    gain_real = jnp.swapaxes(gains[0], 1, 2)[:, :, :, None]
    gain_imag = jnp.swapaxes(gains[1], 1, 2)[:, :, :, None]
    real_part = spectra[0] * gain_real - spectra[1] * gain_imag
    imag_part = spectra[0] * gain_imag + spectra[1] * gain_real
    outgoing = jnp.stack([real_part, imag_part]).astype(jnp.bfloat16)
    outgoing = outgoing.reshape(2, coarse * FINE, local_inputs, frames)
    turned = lax.all_to_all(outgoing, "inp", split_axis=1, concat_axis=2, tiled=True)
    inputs = turned.shape[2]
    span_count = lax.axis_size("span")
    row_count = inputs // span_count
    frame_scale = 1.0 / (span_count * frames)
    row_start = lax.axis_index("span") * row_count
    frame_piece = lax.all_gather(turned, "span", axis=3, tiled=True)
    left_all = jnp.concatenate([frame_piece[0], frame_piece[1]], axis=-1)
    own_rows = lax.dynamic_slice_in_dim(frame_piece, row_start, row_count, 2)
    left_rows = jnp.concatenate([own_rows[0], own_rows[1]], axis=-1)
    right_rows = jnp.concatenate([own_rows[1], -own_rows[0]], axis=-1)
    summed = packed_rows(left_rows, right_rows, left_all, row_start) * frame_scale
    return summed.astype(jnp.bfloat16)


def solution(mesh):
    placed = (P(None, "beam", "inp", "span"), P(None, "beam", "inp", None))
    return jax.shard_map(
        local,
        mesh=mesh,
        in_specs=placed,
        out_specs=P(("beam", "inp"), "span", None),
        check_vma=False,
    )
```

profile of v0, /device:TPU:0, one launch (start us, length us, event | category | flops | bytes accessed | tf_op | source)
XLA Modules:
  0.0 864.3 jit_solution(2377499240589222631)
XLA Ops:
  6.5 0.0 all-gather.2.cloned.1.call-start
  6.5 0.7 multiply_reduce_fusion
  7.9 0.1 fusion.45
  8.0 21.2 %copy.28 = bf16[2,4,128,8192]{2,3,1,0:T(8,128)(2,1)} copy(bf16[2,4,128,8192]{3,2,1,0:T(8,128)(2,1)} %param.2) | data formatting | bytes 33554432 | tf_op args[0]
  29.2 32.5 %pad_slice_fusion.2 = (bf16[2,4,128,8192]{2,3,1,0:T(8,128)(2,1)}, bf16[2,4,128,8192]{2,3,1,0:T(8,128)(2,1)}, bf16[2,4,128,8192]{2,3,1,0:T(8,128)(2,1)}) fusion(bf16[2,4,128,8192]{2,3,1,0:T(8,128)(2,1)} %copy.28), kind=kLoop, calls=%fused_computation.22 | loop fusion | bytes 67108864 | tf_op jit(solution)/shard_map/slice | solution.py:57
  61.6 30.6 %copy.31 = bf16[2,1,4,128,256,32]{4,5,1,0,3,2:T(8,128)(2,1)} copy(bf16[2,1,4,128,256,32]{3,5,4,2,0,1:T(8,128)(2,1)} %bitcast.137) | data formatting | bytes 33554432 | tf_op jit(solution)/shard_map/stack | solution.py:56
  92.3 30.7 %copy.32 = bf16[2,1,4,128,256,32]{4,5,1,0,3,2:T(8,128)(2,1)} copy(bf16[2,1,4,128,256,32]{3,5,4,2,0,1:T(8,128)(2,1)} %bitcast.136) | data formatting | bytes 33554432 | tf_op jit(solution)/shard_map/stack | solution.py:56
  122.9 30.7 %copy.33 = bf16[2,1,4,128,256,32]{4,5,1,0,3,2:T(8,128)(2,1)} copy(bf16[2,1,4,128,256,32]{3,5,4,2,0,1:T(8,128)(2,1)} %bitcast.135) | data formatting | bytes 33554432 | tf_op jit(solution)/shard_map/stack | solution.py:56
  153.6 30.7 %copy.30 = bf16[2,1,4,128,256,32]{4,5,1,0,3,2:T(8,128)(2,1)} copy(bf16[2,1,4,128,256,32]{3,5,4,2,0,1:T(8,128)(2,1)} %bitcast.132) | data formatting | bytes 33554432 | tf_op jit(solution)/shard_map/stack | solution.py:56
  184.2 0.1 fusion.29
  184.4 0.1 fusion.31
  184.6 36.7 %fusion.1 = f32[2,32,4,128,256,1,1]{4,1,6,5,3,2,0:T(8,128)} fusion(bf16[2,1,4,128,256,32]{4,5,1,0,3,2:T(8,128)(2,1)} %copy.33, bf16[2,1,4,128,256,32]{4,5,1,0,3,2:T(8,128)(2,1)} %copy.32, bf16[2,1,4,128,256,32]{4,5,1,0,3,2:T(8,128)(2,1)} %copy.31, bf16[2,1,4,128,256,32]{4,5,1,0,3,2:T(8,128)(2,1)} %copy.30, ...), kind=kOutput, calls=%fused_computation.5 | convolution fusion | flops 4563521536 | bytes 100728832 | tf_op jit(solution)/shard_map/atcnmp,atpbk->bcknm/dot_general | solution.py:64
  221.2 0.0 copy-start
  221.2 44.4 %fusion = f32[2,4,32,128,256]{4,2,3,1,0:T(8,128)} fusion(f32[2,32,4,128,256,1,1]{4,1,6,5,3,2,0:T(8,128)} %fusion.1, bf16[2,1,4,128,256,32]{4,5,1,0,3,2:T(8,128)(2,1)} %copy.33, bf16[2,1,4,128,256,32]{4,5,1,0,3,2:T(8,128)(2,1)} %copy.32, bf16[2,1,4,128,256,32]{4,5,1,0,3,2:T(8,128)(2,1)} %copy.31, bf16[2,1,4,128,256,32]{4,5,1,0,3,2:T(8,128)(2,1)} %copy.30, ...), kind=kOutput, calls=%fused_computation.3 | convolution fusion | flops 4571926528 | bytes 134283264 | tf_op jit(solution)/shard_map/atcnmp,atpbk->bcknm/dot_general | solution.py:61
  265.7 0.0 copy-done
  265.7 0.1 copy.34
  265.8 0.1 copy.35
  265.9 17.8 %subtract_convert_fusion = (bf16[1,4,32,128,256]{4,2,3,1,0:T(8,128)(2,1)}, bf16[1,4,32,128,256]{4,2,3,1,0:T(8,128)(2,1)}) fusion(f32[2,4,32,128,256]{4,2,3,1,0:T(8,128)} %fusion, f32[4,32,128]{1,2,0:T(8,128)S(1)} %copy.35, f32[4,32,128]{1,2,0:T(8,128)S(1)} %copy.34), kind=kLoop, calls=%fused_computation.19 | loop fusion | flops 33554432 | bytes 50462720 | tf_op jit(solution)/shard_map/convert.3
  283.8 11.5 %copy.36 = bf16[1,4,32,128,256]{4,3,2,1,0:T(8,128)(2,1)} copy(bf16[1,4,32,128,256]{4,2,3,1,0:T(8,128)(2,1)} %get-tuple-element.7) | data formatting | bytes 16777216 | tf_op jit(solution)/shard_map/convert.3
  295.2 11.6 %copy.37 = bf16[1,4,32,128,256]{4,3,2,1,0:T(8,128)(2,1)} copy(bf16[1,4,32,128,256]{4,2,3,1,0:T(8,128)(2,1)} %get-tuple-element.8) | data formatting | bytes 16777216 | tf_op jit(solution)/shard_map/convert.2
  306.9 8.0 pad_maximum_fusion.3
  314.9 2.0 copy.38
  316.9 369.9 %all_to_all.18 = bf16[2,128,128,256]{3,2,0,1:T(8,128)(2,1)S(1)} all-to-all(bf16[2,128,128,256]{3,2,0,1:T(8,128)(2,1)S(1)} %copy.38), channel_id=1, replica_groups=mesh['beam'=2,'inp'=8,'span'=2] {'inp'}, dimensions={1} | all-to-all | bytes 33554432 | tf_op jit(solution)/shard_map/all_to_all | solution.py:73
  686.8 6.5 copy.40
  693.3 0.0 all-gather.2.cloned.1.call-update
  693.3 0.4 iota_compare_fusion
  693.7 49.8 %all-gather.2.cloned.1.call-done = bf16[2,16,1024,512]{3,2,1,0:T(8,128)(2,1)} async-done(((bf16[2,16,1024,256]{3,2,1,0:T(8,128)(2,1)}), bf16[2,16,1024,512]{3,2,1,0:T(8,128)(2,1)}) %all-gather.2.cloned.1.call-update) | async-done | bytes 33554448 | tf_op jit(solution)/shard_map/all_gather | solution.py:79
  743.5 22.5 %slice_bitcast_fusion.1 = (bf16[16,1024,512]{2,1,0:T(8,128)(2,1)}, bf16[16,1024,512]{2,1,0:T(8,128)(2,1)}) fusion(bf16[2,16,1024,512]{3,2,1,0:T(8,128)(2,1)} %all-gather.2.cloned.1.call-done), kind=kLoop, calls=%fused_computation.10 | loop fusion | bytes 67108864 | tf_op jit(solution)/shard_map/squeeze | solution.py:80
  765.9 10.3 %fusion.44 = (bf16[16,512,512]{2,1,0:T(8,128)(2,1)}, bf16[16,512,512]{2,1,0:T(8,128)(2,1)}) fusion(bf16[2,16,1024,512]{3,2,1,0:T(8,128)(2,1)} %all-gather.2.cloned.1.call-done, s32[]{:T(128)S(6)} %select_n.117), kind=kLoop, calls=%fused_computation.91 | loop fusion | flops 12582912 | bytes 25165828 | tf_op jit(solution)/shard_map/neg | solution.py:83
  776.2 7.4 dynamic-slice_bitcast_fusion
  783.6 36.8 %fusion.3 = f32[16,512,1024]{2,1,0:T(8,128)} fusion(bf16[16,1024,512]{2,1,0:T(8,128)(2,1)} %get-tuple-element.10, bf16[16,1024,512]{2,1,0:T(8,128)(2,1)} %get-tuple-element.9, bf16[16,512,512]{2,1,0:T(8,128)(2,1)} %get-tuple-element.5, bf16[16,512,512]{2,1,0:T(8,128)(2,1)} %dynamic-slice_bitcast_fusion), kind=kOutput, calls=%fused_computation.7 | convolution fusion | flops 17280532480 | bytes 83886080 | tf_op jit(solution)/shard_map/cif,cjf->cij/dot_general | solution.py:38
  820.5 37.0 %multiply_convert_fusion = bf16[16,512,1024]{2,1,0:T(8,128)(2,1)} fusion(f32[16,512,1024]{2,1,0:T(8,128)} %fusion.3, pred[512,1024]{1,0:T(8,128)(4,1)S(1)} %iota_compare_fusion, bf16[16,1024,512]{2,1,0:T(8,128)(2,1)} %get-tuple-element.10, bf16[16,1024,512]{2,1,0:T(8,128)(2,1)} %get-tuple-element.9, bf16[16,512,512]{2,1,0:T(8,128)(2,1)} %dynamic-slice_bitcast_fusion, ...), kind=kOutput, calls=%fused_computation.4 | convolution fusion | flops 17305698304 | bytes 101187584 | tf_op jit(solution)/shard_map/cif,cjf->cij/dot_general | solution.py:37
  (10 shorter events, 0.1 us)
Async XLA Ops:
  6.5 736.9 %all-gather.2.cloned.1.call-start = ((), (), s32[]{:S(2)}) async-start(), calls=%async_computation.1 | async-start | bytes 50331648 | tf_op jit(solution)/shard_map/all_gather | solution.py:79
  221.2 44.4 %copy-start = (f32[2,4,128,32]{2,3,1,0:T(8,128)S(1)}, f32[2,4,128,32]{2,3,1,0:T(8,128)}, u32[]{:S(2)}) copy-start(f32[2,4,128,32]{2,3,1,0:T(8,128)} %param.3) | copy-start | bytes 393220
Sparse Core Ops, SparseCore 0:
  693.4 49.9 all-gather.1
where the time goes:
time: 868 us; the launch traced here: 864 us
  blocking collectives  370 us (43%)
  local copies, waits for them, and re-layouts  238 us (27%)
  matrix products  155 us (18%)
  waiting for transfers between devices  49.8 us (6%)
  other arithmetic  37.4 us (4%)
  between operations  14.2 us (2%)
    all_to_all x1, blocking collectives, local(): lax.all_to_all(outgoing, 'inp', split_axis=1, concat_axis=2, tiled=True)  370 us
    another operation x4, local copies, waits for them, and re-layouts, local(): jnp.stack([padded[..., tap_index * FINE:tap_index * FINE + samples] for t...  123 us
    all_gather x1, waiting for transfers between devices, local(): frame_piece = lax.all_gather(turned, 'span', axis=3, tiled=True)  49.8 us
    dot_general x1, matrix products, local(): jnp.einsum('atcnmp,atpbk->bcknm', stacked, filter_high, preferred_element...  44.4 us
    dot_general x1, matrix products, packed_rows(): jnp.einsum('cif,cjf->cij', left_rows, left_all, preferred_element_type=jn...  37 us
    dot_general x1, matrix products, packed_rows(): jnp.einsum('cif,cjf->cij', right_rows, left_all, preferred_element_type=j...  36.8 us
    dot_general x1, matrix products, local(): jnp.einsum('atcnmp,atpbk->bcknm', stacked, filter_low, preferred_element_...  36.7 us
    slice x1, local copies, waits for them, and re-layouts, local(): padded[..., tap_index * FINE:tap_index * FINE + samples]  32.5 us
  transfers between devices with their start and end apart: 1, of which 1 were waited for; matrix products, arithmetic and copies ran while one was open for 0% of the time, Pallas kernels for 0%

commit v1 on v0

--- a/solution.py
+++ b/solution.py
@@ -6,6 +6,29 @@
 
 FINE = 32
 TAPS = 4
+
+
+def split_up(shard, dim, size):
+    dims = shard.shape
+    blocks = shard.reshape(*dims[:dim], size, dims[dim] // size, *dims[dim + 1 :])
+    return jnp.moveaxis(blocks, dim, 0)
+
+
+def in_order(blocks, dim):
+    lengths = list(blocks.shape[1:])
+    lengths[dim] *= blocks.shape[0]
+    return jnp.moveaxis(blocks, 0, dim).reshape(lengths)
+
+
+def swapped_with_each(x, axis, split_dim, concat_dim):
+    size, index = (lax.axis_size(axis), lax.axis_index(axis))
+    pieces = split_up(x, split_dim, size)
+    gathered = [pieces[index]]
+    for hop in range(1, size):
+        sent = pieces[index ^ hop]
+        gathered.append(lax.ppermute(sent, axis, [(i, i ^ hop) for i in range(size)]))
+    pieces = jnp.stack(gathered)[index ^ jnp.arange(size)]
+    return in_order(pieces, concat_dim)
 
 
 def prototype(tap_count, fine_count):
@@ -70,7 +93,7 @@
     imag_part = spectra[0] * gain_imag + spectra[1] * gain_real
     outgoing = jnp.stack([real_part, imag_part]).astype(jnp.bfloat16)
     outgoing = outgoing.reshape(2, coarse * FINE, local_inputs, frames)
-    turned = lax.all_to_all(outgoing, "inp", split_axis=1, concat_axis=2, tiled=True)
+    turned = swapped_with_each(outgoing, "inp", 1, 2)
     inputs = turned.shape[2]
     span_count = lax.axis_size("span")
     row_count = inputs // span_count

time: 868 us -> 897 us (1.033)
  blocking collectives: 370 us -> 0 us
  waiting for transfers between devices: 49.8 us -> 389 us
  local copies, waits for them, and re-layouts: 238 us -> 270 us
  starting transfers between devices: 0.01 us -> 13.8 us
  other arithmetic: 37.4 us -> 50.8 us
    all_to_all x1 -> x0, blocking collectives: 370 us -> none  [local(): lax.all_to_all(outgoing, 'inp', split_axis=1, concat_axis=2, tiled=True)]
    ppermute x0 -> x7, waiting for transfers between devices: none -> 255 us  [swapped_with_each(): lax.ppermute(sent, axis, [(i, i ^ hop) for i in range(size)])]
    all_gather x1, waiting for transfers between devices: 49.8 us -> 134 us  [local(): frame_piece = lax.all_gather(turned, 'span', axis=3, tiled=True)]
    gather x0 -> x3, local copies, waits for them, and re-layouts: none -> 23.4 us  [swapped_with_each(): pieces = jnp.stack(gathered)[index ^ jnp.arange(size)]]
    ppermute x0 -> x7, starting transfers between devices: none -> 13.7 us  [swapped_with_each(): lax.ppermute(sent, axis, [(i, i ^ hop) for i in range(size)])]
    squeeze x0 -> x2, other arithmetic: none -> 11.3 us  [swapped_with_each(): sent = pieces[index ^ hop]]
    unnamed x3 -> x9, local copies, waits for them, and re-layouts: 21.2 us -> 32 us
    another operation x2 -> x1, other arithmetic: 25.8 us -> 17.9 us
  transfers between devices with their start and end apart: 1 -> 8, of which waited for: 1 -> 5; matrix products, arithmetic and copies ran while one was open for 0% -> 2% of each run, Pallas kernels for 0% -> 0%
where the time goes in v1:
time: 897 us; the launch traced here: 893 us
  waiting for transfers between devices  389 us (43%)
  local copies, waits for them, and re-layouts  270 us (30%)
  matrix products  155 us (17%)
  other arithmetic  50.8 us (6%)
  between operations  14.3 us (2%)
  starting transfers between devices  13.8 us (2%)
    ppermute x7, waiting for transfers between devices, swapped_with_each(): lax.ppermute(sent, axis, [(i, i ^ hop) for i in range(size)])  255 us
    all_gather x1, waiting for transfers between devices, local(): frame_piece = lax.all_gather(turned, 'span', axis=3, tiled=True)  134 us
    another operation x4, local copies, waits for them, and re-layouts, local(): jnp.stack([padded[..., tap_index * FINE:tap_index * FINE + samples] for t...  123 us
    dot_general x1, matrix products, local(): jnp.einsum('atcnmp,atpbk->bcknm', stacked, filter_high, preferred_element...  44.4 us
    dot_general x1, matrix products, packed_rows(): jnp.einsum('cif,cjf->cij', left_rows, left_all, preferred_element_type=jn...  36.9 us
    dot_general x1, matrix products, packed_rows(): jnp.einsum('cif,cjf->cij', right_rows, left_all, preferred_element_type=j...  36.9 us
    dot_general x1, matrix products, local(): jnp.einsum('atcnmp,atpbk->bcknm', stacked, filter_low, preferred_element_...  36.7 us
    slice x1, local copies, waits for them, and re-layouts, local(): padded[..., tap_index * FINE:tap_index * FINE + samples]  32.5 us
  transfers between devices with their start and end apart: 8, of which 5 were waited for; matrix products, arithmetic and copies ran while one was open for 2% of the time, Pallas kernels for 0%

profile of v1, /device:TPU:0, one launch (start us, length us, event | category | flops | bytes accessed | tf_op | source)
XLA Modules:
  0.0 893.2 jit_solution(10771357685623179973)
XLA Ops:
  6.5 0.0 all-gather.2.cloned.1.call-start
  6.5 0.7 multiply_reduce_fusion
  7.9 0.1 fusion.62
  8.0 21.2 %copy.13 = bf16[2,4,128,8192]{2,3,1,0:T(8,128)(2,1)} copy(bf16[2,4,128,8192]{3,2,1,0:T(8,128)(2,1)} %param.2) | data formatting | bytes 33554432 | tf_op args[0]
  29.2 32.5 %pad_slice_fusion.2 = (bf16[2,4,128,8192]{2,3,1,0:T(8,128)(2,1)}, bf16[2,4,128,8192]{2,3,1,0:T(8,128)(2,1)}, bf16[2,4,128,8192]{2,3,1,0:T(8,128)(2,1)}) fusion(bf16[2,4,128,8192]{2,3,1,0:T(8,128)(2,1)} %copy.13), kind=kLoop, calls=%fused_computation.40 | loop fusion | bytes 67108864 | tf_op jit(solution)/shard_map/slice | solution.py:80
  61.7 30.6 %copy.16 = bf16[2,1,4,128,256,32]{4,5,1,0,3,2:T(8,128)(2,1)} copy(bf16[2,1,4,128,256,32]{3,5,4,2,0,1:T(8,128)(2,1)} %bitcast.173) | data formatting | bytes 33554432 | tf_op jit(solution)/shard_map/stack | solution.py:79
  92.3 30.7 %copy.17 = bf16[2,1,4,128,256,32]{4,5,1,0,3,2:T(8,128)(2,1)} copy(bf16[2,1,4,128,256,32]{3,5,4,2,0,1:T(8,128)(2,1)} %bitcast.172) | data formatting | bytes 33554432 | tf_op jit(solution)/shard_map/stack | solution.py:79
  123.0 30.6 %copy.18 = bf16[2,1,4,128,256,32]{4,5,1,0,3,2:T(8,128)(2,1)} copy(bf16[2,1,4,128,256,32]{3,5,4,2,0,1:T(8,128)(2,1)} %bitcast.171) | data formatting | bytes 33554432 | tf_op jit(solution)/shard_map/stack | solution.py:79
  153.6 30.6 %copy.15 = bf16[2,1,4,128,256,32]{4,5,1,0,3,2:T(8,128)(2,1)} copy(bf16[2,1,4,128,256,32]{3,5,4,2,0,1:T(8,128)(2,1)} %bitcast.163) | data formatting | bytes 33554432 | tf_op jit(solution)/shard_map/stack | solution.py:79
  184.2 0.1 fusion.46
  184.4 0.1 fusion.44
  184.6 36.7 %fusion.1 = f32[2,32,4,128,256,1,1]{4,1,6,5,3,2,0:T(8,128)} fusion(bf16[2,1,4,128,256,32]{4,5,1,0,3,2:T(8,128)(2,1)} %copy.18, bf16[2,1,4,128,256,32]{4,5,1,0,3,2:T(8,128)(2,1)} %copy.17, bf16[2,1,4,128,256,32]{4,5,1,0,3,2:T(8,128)(2,1)} %copy.16, bf16[2,1,4,128,256,32]{4,5,1,0,3,2:T(8,128)(2,1)} %copy.15, ...), kind=kOutput, calls=%fused_computation.23 | convolution fusion | flops 4563521536 | bytes 100728832 | tf_op jit(solution)/shard_map/atcnmp,atpbk->bcknm/dot_general | solution.py:87
  221.3 0.0 copy-start
  221.3 44.4 %fusion = f32[2,4,32,128,256]{4,2,3,1,0:T(8,128)} fusion(f32[2,32,4,128,256,1,1]{4,1,6,5,3,2,0:T(8,128)} %fusion.1, bf16[2,1,4,128,256,32]{4,5,1,0,3,2:T(8,128)(2,1)} %copy.18, bf16[2,1,4,128,256,32]{4,5,1,0,3,2:T(8,128)(2,1)} %copy.17, bf16[2,1,4,128,256,32]{4,5,1,0,3,2:T(8,128)(2,1)} %copy.16, bf16[2,1,4,128,256,32]{4,5,1,0,3,2:T(8,128)(2,1)} %copy.15, ...), kind=kOutput, calls=%fused_computation.5 | convolution fusion | flops 4571926528 | bytes 134283264 | tf_op jit(solution)/shard_map/atcnmp,atpbk->bcknm/dot_general | solution.py:84
  265.7 0.0 copy-done
  265.7 0.1 copy.19
  265.8 0.1 copy.20
  266.0 17.9 %subtract_convert_fusion = (bf16[1,4,32,128,256]{4,2,3,1,0:T(8,128)(2,1)}, bf16[1,4,32,128,256]{4,2,3,1,0:T(8,128)(2,1)}) fusion(f32[2,4,32,128,256]{4,2,3,1,0:T(8,128)} %fusion, f32[4,32,128]{1,2,0:T(8,128)S(1)} %copy.20, f32[4,32,128]{1,2,0:T(8,128)S(1)} %copy.19), kind=kLoop, calls=%fused_computation.37 | loop fusion | flops 33554432 | bytes 50462720 | tf_op jit(solution)/shard_map/convert.3
  283.8 11.5 %copy.21 = bf16[1,4,32,128,256]{4,3,2,1,0:T(8,128)(2,1)} copy(bf16[1,4,32,128,256]{4,2,3,1,0:T(8,128)(2,1)} %get-tuple-element.7) | data formatting | bytes 16777216 | tf_op jit(solution)/shard_map/convert.3
  295.3 11.6 %copy.22 = bf16[1,4,32,128,256]{4,3,2,1,0:T(8,128)(2,1)} copy(bf16[1,4,32,128,256]{4,2,3,1,0:T(8,128)(2,1)} %get-tuple-element.8) | data formatting | bytes 16777216 | tf_op jit(solution)/shard_map/convert.2
  307.0 8.2 fusion.27
  315.2 3.0 collective-permute-start
  318.2 1.6 collective-permute-start.1
  319.8 0.0 collective-permute-start.2
  319.8 3.0 collective-permute-start.3
  322.8 1.3 collective-permute-start.4
  324.1 3.0 fusion.21
  327.1 37.1 %collective-permute-done = bf16[2,16,128,256]{3,2,1,0:T(8,128)(2,1)} collective-permute-done((bf16[2,16,128,256]{3,2,1,0:T(8,128)(2,1)}, bf16[2,16,128,256]{3,2,1,0:T(8,128)(2,1)}, u32[]{:S(2)}, u32[]{:S(2)}) %collective-permute-start) | collective-permute-done | bytes 2097184 | tf_op jit(solution)/shard_map/ppermute | solution.py:29
  364.2 3.8 collective-permute-start.5
  368.0 1.7 bitcast_dynamic-update-slice_fusion.7
  369.8 86.2 %collective-permute-done.1 = bf16[2,16,128,256]{3,2,1,0:T(8,128)(2,1)} collective-permute-done((bf16[2,16,128,256]{3,2,1,0:T(8,128)(2,1)}, bf16[2,16,128,256]{3,2,1,0:T(8,128)(2,1)}, u32[]{:S(2)}, u32[]{:S(2)}) %collective-permute-start.1) | collective-permute-done | bytes 2097184 | tf_op jit(solution)/shard_map/ppermute | solution.py:29
  456.0 1.0 collective-permute-start.6
  457.1 1.8 bitcast_dynamic-update-slice_fusion.6
  458.9 1.8 bitcast_dynamic-update-slice_fusion.5
  460.7 38.0 %collective-permute-done.2 = bf16[2,16,128,256]{3,2,1,0:T(8,128)(2,1)} collective-permute-done((bf16[2,16,128,256]{3,2,1,0:T(8,128)(2,1)}, bf16[2,16,128,256]{3,2,1,0:T(8,128)(2,1)}, u32[]{:S(2)}, u32[]{:S(2)}) %collective-permute-start.2) | collective-permute-done | bytes 2097184 | tf_op jit(solution)/shard_map/ppermute | solution.py:29
  498.7 1.8 bitcast_dynamic-update-slice_fusion.4
  500.5 0.0 collective-permute-done.3
  500.5 1.8 bitcast_dynamic-update-slice_fusion.3
  502.3 93.3 %collective-permute-done.4 = bf16[2,16,128,256]{3,2,1,0:T(8,128)(2,1)} collective-permute-done((bf16[2,16,128,256]{3,2,1,0:T(8,128)(2,1)}, bf16[2,16,128,256]{3,2,1,0:T(8,128)(2,1)}, u32[]{:S(2)}, u32[]{:S(2)}) %collective-permute-start.4) | collective-permute-done | bytes 2097184 | tf_op jit(solution)/shard_map/ppermute | solution.py:29
  595.6 1.8 bitcast_dynamic-update-slice_fusion.2
  597.4 0.0 collective-permute-done.5
  597.4 1.8 bitcast_dynamic-update-slice_fusion.1
  599.2 0.0 collective-permute-done.6
  599.2 0.1 bitcast_dynamic-update-slice_fusion
  599.4 7.1 fusion.61
  606.4 8.1 gather_fusion
  614.5 8.2 gather_fusion.1
  622.7 8.4 maximum_bitcast_fusion.5
  631.1 6.5 copy.23
  637.6 0.0 all-gather.2.cloned.1.call-update
  637.7 0.4 iota_compare_fusion
  638.0 134.4 %all-gather.2.cloned.1.call-done = bf16[2,16,1024,512]{3,2,1,0:T(8,128)(2,1)} async-done(((bf16[2,16,1024,256]{3,2,1,0:T(8,128)(2,1)}), bf16[2,16,1024,512]{3,2,1,0:T(8,128)(2,1)}) %all-gather.2.cloned.1.call-update) | async-done | bytes 33554448 | tf_op jit(solution)/shard_map/all_gather | solution.py:102
  772.4 22.5 %slice_bitcast_fusion.1 = (bf16[16,1024,512]{2,1,0:T(8,128)(2,1)}, bf16[16,1024,512]{2,1,0:T(8,128)(2,1)}) fusion(bf16[2,16,1024,512]{3,2,1,0:T(8,128)(2,1)} %all-gather.2.cloned.1.call-done), kind=kLoop, calls=%fused_computation.28 | loop fusion | bytes 67108864 | tf_op jit(solution)/shard_map/squeeze | solution.py:103
  794.9 10.3 %fusion.60 = (bf16[16,512,512]{2,1,0:T(8,128)(2,1)}, bf16[16,512,512]{2,1,0:T(8,128)(2,1)}) fusion(bf16[2,16,1024,512]{3,2,1,0:T(8,128)(2,1)} %all-gather.2.cloned.1.call-done, s32[]{:T(128)S(6)} %select_n.160), kind=kLoop, calls=%fused_computation.135 | loop fusion | flops 12582912 | bytes 25165828 | tf_op jit(solution)/shard_map/neg | solution.py:106
  805.2 7.4 dynamic-slice_bitcast_fusion
  812.6 36.9 %fusion.3 = f32[16,512,1024]{2,1,0:T(8,128)} fusion(bf16[16,1024,512]{2,1,0:T(8,128)(2,1)} %get-tuple-element.10, bf16[16,1024,512]{2,1,0:T(8,128)(2,1)} %get-tuple-element.9, bf16[16,512,512]{2,1,0:T(8,128)(2,1)} %get-tuple-element.5, bf16[16,512,512]{2,1,0:T(8,128)(2,1)} %dynamic-slice_bitcast_fusion), kind=kOutput, calls=%fused_computation.25 | convolution fusion | flops 17280532480 | bytes 83886080 | tf_op jit(solution)/shard_map/cif,cjf->cij/dot_general | solution.py:61
  849.5 36.9 %multiply_convert_fusion = bf16[16,512,1024]{2,1,0:T(8,128)(2,1)} fusion(f32[16,512,1024]{2,1,0:T(8,128)} %fusion.3, pred[512,1024]{1,0:T(8,128)(4,1)S(1)} %iota_compare_fusion, bf16[16,1024,512]{2,1,0:T(8,128)(2,1)} %get-tuple-element.10, bf16[16,1024,512]{2,1,0:T(8,128)(2,1)} %get-tuple-element.9, bf16[16,512,512]{2,1,0:T(8,128)(2,1)} %dynamic-slice_bitcast_fusion, ...), kind=kOutput, calls=%fused_computation.6 | convolution fusion | flops 17305698304 | bytes 101187584 | tf_op jit(solution)/shard_map/cif,cjf->cij/dot_general | solution.py:60
  (12 shorter events, 0.1 us)
Async XLA Ops:
  6.5 765.9 %all-gather.2.cloned.1.call-start = ((), (), s32[]{:S(2)}) async-start(), calls=%async_computation | async-start | bytes 50331648 | tf_op jit(solution)/shard_map/all_gather | solution.py:102
  221.3 44.4 %copy-start = (f32[2,4,128,32]{2,3,1,0:T(8,128)S(1)}, f32[2,4,128,32]{2,3,1,0:T(8,128)}, u32[]{:S(2)}) copy-start(f32[2,4,128,32]{2,3,1,0:T(8,128)} %param.3) | copy-start | bytes 393220
  315.2 49.0 %collective-permute-start = (bf16[2,16,128,256]{3,2,1,0:T(8,128)(2,1)}, bf16[2,16,128,256]{3,2,1,0:T(8,128)(2,1)}, u32[]{:S(2)}, u32[]{:S(2)}) collective-permute-start(bf16[2,16,128,256]{3,2,1,0:T(8,128)(2,1)} %get-tuple-element.14), channel_id=1, source_target_pairs={{0,2},{2,0},{4,6},{6,4},{8,10},{10,8},{12,14},{14,12},{1,3},{3,1},... | collective-permute-start | bytes 6291464 | tf_op jit(solution)/shard_map/ppermute | solution.py:29
  318.2 137.8 %collective-permute-start.1 = (bf16[2,16,128,256]{3,2,1,0:T(8,128)(2,1)}, bf16[2,16,128,256]{3,2,1,0:T(8,128)(2,1)}, u32[]{:S(2)}, u32[]{:S(2)}) collective-permute-start(bf16[2,16,128,256]{3,2,1,0:T(8,128)(2,1)} %get-tuple-element.15), channel_id=1, source_target_pairs={{0,4},{2,6},{4,0},{6,2},{8,12},{10,14},{12,8},{14,10},{1,5},{3,7},... | collective-permute-start | bytes 6291464 | tf_op jit(solution)/shard_map/ppermute | solution.py:29
  319.8 178.9 %collective-permute-start.2 = (bf16[2,16,128,256]{3,2,1,0:T(8,128)(2,1)}, bf16[2,16,128,256]{3,2,1,0:T(8,128)(2,1)}, u32[]{:S(2)}, u32[]{:S(2)}) collective-permute-start(bf16[2,16,128,256]{3,2,1,0:T(8,128)(2,1)} %get-tuple-element.16), channel_id=1, source_target_pairs={{0,6},{2,4},{4,2},{6,0},{8,14},{10,12},{12,10},{14,8},{1,7},{3,5},... | collective-permute-start | bytes 6291464 | tf_op jit(solution)/shard_map/ppermute | solution.py:29
  319.8 180.7 %collective-permute-start.3 = (bf16[2,16,128,256]{3,2,1,0:T(8,128)(2,1)}, bf16[2,16,128,256]{3,2,1,0:T(8,128)(2,1)}, u32[]{:S(2)}, u32[]{:S(2)}) collective-permute-start(bf16[2,16,128,256]{3,2,1,0:T(8,128)(2,1)} %get-tuple-element.17), channel_id=1, source_target_pairs={{0,8},{2,10},{4,12},{6,14},{8,0},{10,2},{12,4},{14,6},{1,9},{3,11}... | collective-permute-start | bytes 6291464 | tf_op jit(solution)/shard_map/ppermute | solution.py:29
  322.8 272.8 %collective-permute-start.4 = (bf16[2,16,128,256]{3,2,1,0:T(8,128)(2,1)}, bf16[2,16,128,256]{3,2,1,0:T(8,128)(2,1)}, u32[]{:S(2)}, u32[]{:S(2)}) collective-permute-start(bf16[2,16,128,256]{3,2,1,0:T(8,128)(2,1)} %get-tuple-element.18), channel_id=1, source_target_pairs={{0,10},{2,8},{4,14},{6,12},{8,2},{10,0},{12,6},{14,4},{1,11},{3,9}... | collective-permute-start | bytes 6291464 | tf_op jit(solution)/shard_map/ppermute | solution.py:29
  364.2 233.2 %collective-permute-start.5 = (bf16[2,16,128,256]{3,2,1,0:T(8,128)(2,1)}, bf16[2,16,128,256]{3,2,1,0:T(8,128)(2,1)}, u32[]{:S(2)}, u32[]{:S(2)}) collective-permute-start(bf16[2,16,128,256]{3,2,1,0:T(8,128)(2,1)} %fusion.21), channel_id=1, source_target_pairs={{0,12},{2,14},{4,8},{6,10},{8,4},{10,6},{12,0},{14,2},{1,13},{3,15... | collective-permute-start | bytes 6291464 | tf_op jit(solution)/shard_map/ppermute | solution.py:29
  456.0 143.2 %collective-permute-start.6 = (bf16[2,16,128,256]{3,2,1,0:T(8,128)(2,1)S(1)}, bf16[2,16,128,256]{3,2,1,0:T(8,128)(2,1)S(1)}, u32[]{:S(2)}, u32[]{:S(2)}) collective-permute-start(bf16[2,16,128,256]{3,2,1,0:T(8,128)(2,1)S(1)} %get-tuple-element.13), channel_id=1, source_target_pairs={{0,14},{2,12},{4,10},{6,8},{8,6},{10,4},{12,2},{14,0},{1,15},{3,13... | collective-permute-start | bytes 6291464 | tf_op jit(solution)/shard_map/ppermute | solution.py:29
Sparse Core Ops, SparseCore 0:
  637.8 134.6 all-gather.1
